TPU v7x, 32 devices: a whole 2x2x4 slice. The times are simulated.
32 devices in a mesh: section: 8 (over y, x, core), tensor: 4 (over z).
Axes of the slice: x: 2, y: 2, z: 4, core: 2. Of those that a mesh axis runs over, the one named last changes fastest.
Arguments:
- acts: bfloat16 [8, 2, 32, 4096], P('section', None, None, 'tensor'), may hold values from -6 to 6
- grads_in: bfloat16 [8, 2, 32, 4096], P('section', None, None, 'tensor'), may hold values from -6 to 6
- head_grads: bfloat16 [8, 2, 128, 512], P('section', None, None, 'tensor'), may hold values from -6 to 6
- types: int32 [8, 2, 32], P('section'), may hold values 0 or 1
- gains: bfloat16 [8, 2, 2, 1024], P('section'), may hold values from 0.3984375 to 1.59375
- w_query: bfloat16 [8, 2, 4096, 512], P('section', None, None, 'tensor'), may hold values from -0.09375 to 0.09375
- w_key: bfloat16 [8, 2, 4096, 128], P('section', None, None, 'tensor'), may hold values from -0.09375 to 0.09375
- w_value: bfloat16 [8, 2, 4096, 128], P('section', None, None, 'tensor'), may hold values from -0.09375 to 0.09375
Outputs:
- routed: bfloat16 [8, 2, 32, 4096], P('section', None, None, 'tensor')
All inputs are finite; a program needn't handle non-finite values. No bound on the sum of `types` on one device may be relied on, other than what follows from the above.
Results may differ from a plain program's by a relative error of at most 0.0055.
Values may be sent and summed in bfloat16 or wider, within the bound.
A program may use at most 64 MiB of HBM per device.

v0:
```python
import jax
import jax.numpy as jnp
from jax import lax
from jax.sharding import PartitionSpec as P

HEAD_DIM = 128
SUB = 4
epsilon = 1e-05


def swapped(value, axis, stride):
    mask = 2**stride
    pairs = [(source, source ^ mask) for source in range(lax.axis_size(axis))]
    return lax.ppermute(value, axis, pairs)


def shifted(value, axis, by):
    peers = lax.axis_size(axis)
    return lax.ppermute(value, axis, [(i, (i + by) % peers) for i in range(peers)])


def sum_columns(first, second):
    return (
        lax.psum_scatter(first, "tensor", scatter_dimension=2, tiled=True),
        lax.psum_scatter(second, "tensor", scatter_dimension=2, tiled=True),
    )


def collect_rows(member, position, levels, axis):
    for bit in range(levels):
        partner = swapped(member, "section", bit)
        upper_bit = position >> bit & 1
        member = jnp.where(
            upper_bit == 1,
            jnp.concatenate([partner, member], axis=axis),
            jnp.concatenate([member, partner], axis=axis),
        )
    return member


def halve_once(member, upper_bit, bit):
    half_rows = member.shape[1] // 2
    lower_rows = member[:, :half_rows]
    higher_rows = member[:, half_rows:]
    kept_rows = jnp.where(upper_bit == 1, higher_rows, lower_rows)
    sent_rows = jnp.where(upper_bit == 1, lower_rows, higher_rows)
    return kept_rows + swapped(sent_rows, "section", bit)


def reduce_rows(first, second, position, levels):
    for bit in reversed(range(levels)):
        upper_bit = position >> bit & 1
        first = halve_once(first, upper_bit, bit)
        second = halve_once(second, upper_bit, bit)
    return (first, second)


def per_device(acts, grads_in, head_grads, types, gains, w_query, w_key, w_value):
    tensors = lax.axis_size("tensor")
    section_count = lax.axis_size("section") // SUB
    levels = SUB.bit_length() - 1
    position = lax.axis_index("section") % SUB
    section_here = lax.axis_index("section") // SUB
    x_local = acts[0]
    grad_local = grads_in[0]
    out_grads = head_grads[0]
    w_query = w_query[0]
    w_key = w_key[0]
    w_value = w_value[0]
    x_cols = lax.all_gather(x_local, "tensor", axis=2, tiled=True)
    x_full = collect_rows(x_cols, position, levels, 1)
    kind_full = collect_rows(types[0].astype(jnp.bfloat16), position, levels, 1)
    gain_full = collect_rows(gains[0], position, levels, 2).astype(jnp.float32)
    tokens = x_full.shape[1]
    tokq = x_local.shape[1]
    width = x_full.shape[2]
    cols_dev = x_local.shape[2]
    x_float = x_full.astype(jnp.float32)
    inverse = lax.rsqrt(jnp.mean(x_float * x_float, axis=-1, keepdims=True) + epsilon)
    gain_rows = jnp.where(kind_full[..., None] > 0.5, gain_full[:, 1:2, :], gain_full[:, 0:1, :])
    normed = (x_float * inverse * gain_rows).astype(jnp.bfloat16)
    queries = jnp.einsum(
        "ctd,cdh->cth", normed, w_query, preferred_element_type=jnp.float32
    ).astype(jnp.bfloat16)
    key_part = jnp.einsum("ctd,cdh->cth", normed, w_key, preferred_element_type=jnp.float32).astype(
        jnp.bfloat16
    )
    value_part = jnp.einsum(
        "ctd,cdh->cth", normed, w_value, preferred_element_type=jnp.float32
    ).astype(jnp.bfloat16)
    key_rows, value_rows = (
        lax.all_gather(key_part, "tensor", axis=2, tiled=True),
        lax.all_gather(value_part, "tensor", axis=2, tiled=True),
    )
    softmax_scale = HEAD_DIM ** (-0.5)
    scores = (
        jnp.einsum("cqh,ckh->cqk", queries, key_rows, preferred_element_type=jnp.float32)
        * softmax_scale
    )
    causal = jnp.arange(tokens)[:, None] >= jnp.arange(tokens)[None, :]
    scores = jnp.where(causal[None], scores, -1e30)
    attn_probs = jax.nn.softmax(scores, axis=-1)
    probs_low = attn_probs.astype(jnp.bfloat16)
    prob_grads = jnp.einsum(
        "cqh,ckh->cqk", out_grads, value_rows, preferred_element_type=jnp.float32
    )
    score_grads = (
        attn_probs
        * (prob_grads - jnp.sum(prob_grads * attn_probs, axis=-1, keepdims=True))
        * softmax_scale
    ).astype(jnp.bfloat16)
    query_grads = jnp.einsum(
        "cqk,ckh->cqh", score_grads, key_rows, preferred_element_type=jnp.float32
    ).astype(jnp.bfloat16)
    key_each = jnp.einsum("cqk,cqh->ckh", score_grads, queries, preferred_element_type=jnp.float32)
    value_each = jnp.einsum(
        "cqk,cqh->ckh", probs_low, out_grads, preferred_element_type=jnp.float32
    )
    key_sum, value_sum = sum_columns(key_each, value_each)
    key_grads = key_sum.astype(jnp.bfloat16)
    value_grads = value_sum.astype(jnp.bfloat16)
    joined_grads = jnp.concatenate([query_grads, key_grads, value_grads], axis=2)
    joined_weights = jnp.concatenate([w_query, w_key, w_value], axis=2)
    partial_value = jnp.einsum(
        "cth,cdh->ctd", joined_grads, joined_weights, preferred_element_type=jnp.float32
    )
    stat_part = jnp.sum(x_float * gain_rows * partial_value, axis=-1)
    stat_wide = jnp.broadcast_to(stat_part[..., None], stat_part.shape + (tensors,))
    grad_rows_sum, stat_rows = reduce_rows(partial_value, stat_wide, position, levels)
    grad_mine, stat_mine = sum_columns(grad_rows_sum, stat_rows)
    my_inverse = lax.dynamic_slice_in_dim(inverse, position * tokq, tokq, 1)
    my_gain = lax.dynamic_slice_in_dim(gain_rows, position * tokq, tokq, 1)
    my_gain = lax.dynamic_slice_in_dim(my_gain, lax.axis_index("tensor") * cols_dev, cols_dev, 2)
    my_x = x_local.astype(jnp.float32)
    stat_mean = stat_mine / width
    norm_grads = my_inverse * my_gain * grad_mine - my_x * my_inverse**3 * stat_mean
    result = (grad_local.astype(jnp.float32) + norm_grads).astype(jnp.bfloat16)
    arrived = shifted(result, "section", -SUB)
    routed = jnp.where(section_here == section_count - 1, arrived[::-1], arrived)
    return routed[None]


def solution(mesh):
    return jax.shard_map(
        per_device,
        mesh=mesh,
        in_specs=(
            P("section", None, None, "tensor"),
            P("section", None, None, "tensor"),
            P("section", None, None, "tensor"),
            P("section", None, None),
            P("section", None, None, None),
            P("section", None, None, "tensor"),
            P("section", None, None, "tensor"),
            P("section", None, None, "tensor"),
        ),
        out_specs=P("section", None, None, "tensor"),
        check_vma=False,
    )
```

profile of v0, /device:TPU:0, one launch (start us, length us, event | category | flops | bytes accessed | tf_op | source)
XLA Modules:
  0.0 225.5 jit_solution(11091461946398277763)
XLA Ops:
  6.5 0.7 convert_bitcast_fusion
  7.3 0.5 collective-permute-start.2
  7.8 0.0 collective-permute-start.4
  7.8 17.7 %all-gather = bf16[1,2,32,4096]{3,2,1,0:T(8,128)(2,1)S(1)} all-gather(bf16[1,2,32,1024]{3,2,1,0:T(8,128)(2,1)} %param.8), channel_id=2, replica_groups=mesh['section'=8,'tensor'=4] {'tensor'}, dimensions={3}, use_global_device_ids=true | all-gather | bytes 655360 | tf_op jit(solution)/shard_map/all_gather | solution.py:70
  25.5 0.1 broadcast_select_fusion.6
  25.6 1.5 collective-permute-start.3
  27.1 0.8 broadcast_select_fusion.2
  27.9 0.6 collective-permute-start.5
  28.5 0.7 collective-permute-done.3
  29.2 0.1 fusion.52
  29.2 2.4 %collective-permute-done.5 = bf16[2,2,2048]{2,1,0:T(2,128)(2,1)S(1)} collective-permute-done((bf16[2,2,2048]{2,1,0:T(2,128)(2,1)S(1)}, bf16[2,2,2048]{2,1,0:T(2,128)(2,1)S(1)}, u32[]{:S(2)}, u32[]{:S(2)}) %collective-permute-start.5) | collective-permute-done | bytes 16416 | tf_op jit(solution)/shard_map/ppermute | solution.py:14
  31.7 0.2 maximum_select_fusion.1
  32.0 0.6 collective-permute-start.1
  32.6 0.1 fusion.60
  32.6 0.1 copy_bitcast_fusion
  32.7 23.5 %collective-permute-done.1 = bf16[2,64,4096]{2,1,0:T(8,128)(2,1)S(1)} collective-permute-done((bf16[2,64,4096]{2,1,0:T(8,128)(2,1)S(1)}, bf16[2,64,4096]{2,1,0:T(8,128)(2,1)S(1)}, u32[]{:S(2)}, u32[]{:S(2)}) %collective-permute-start.1) | collective-permute-done | bytes 1048608 | tf_op jit(solution)/shard_map/ppermute | solution.py:14
  56.2 0.8 fusion.2
  57.0 1.3 convolution_convert_fusion.2
  58.2 13.4 %all_gather.10 = bf16[2,128,128]{1,2,0:T(8,128)(2,1)S(1)} all-gather(bf16[2,128,32]{1,2,0:T(8,128)(2,1)S(1)} %convolution_convert_fusion.2), channel_id=1, replica_groups=mesh['section'=8,'tensor'=4] {'tensor'}, dimensions={2}, use_global_device_ids=true | all-gather | bytes 81920 | tf_op jit(solution)/shard_map/all_gather | solution.py:92
  71.7 1.3 convolution_convert_fusion.1
  72.9 13.2 %all_gather.11 = bf16[2,128,128]{1,2,0:T(8,128)(2,1)S(1)} all-gather(bf16[2,128,32]{1,2,0:T(8,128)(2,1)S(1)} %convolution_convert_fusion.1), channel_id=1, replica_groups=mesh['section'=8,'tensor'=4] {'tensor'}, dimensions={2}, use_global_device_ids=true | all-gather | bytes 81920 | tf_op jit(solution)/shard_map/all_gather | solution.py:93
  86.2 1.4 fusion.22
  87.5 0.2 fusion.18
  87.8 0.7 fusion.61
  88.5 0.9 fusion.43
  89.3 0.0 reduce-scatter.6.cloned.1.call-update
  89.4 0.0 reduce-scatter.4.cloned.1.call-start
  89.4 0.2 convolution_bitcast_fusion
  89.6 1.9 fusion.25
  91.5 0.0 reduce-scatter.4.cloned.1.call-update
  91.5 0.0 reduce-scatter.8.cloned.1.call-start
  91.6 2.8 %copy.11 = bf16[1,2,4096,128]{2,3,1,0:T(8,128)(2,1)} copy(bf16[1,2,4096,128]{3,2,1,0:T(8,128)(2,1)S(1)} %copy-done.1) | data formatting | bytes 4194304 | tf_op args[5]
  94.4 1.2 convolution_convert_fusion
  95.6 13.9 %reduce-scatter.6.cloned.1.call-done = f32[2,128,32]{1,2,0:T(8,128)} async-done(((f32[2,128,128]{1,2,0:T(8,128)}), f32[2,128,32]{1,2,0:T(8,128)}) %reduce-scatter.6.cloned.1.call-update) | async-done | bytes 32784 | tf_op jit(solution)/shard_map/reduce_scatter | solution.py:25
  109.5 0.8 convert_element_type.65
  110.2 19.1 %reduce-scatter.4.cloned.1.call-done = f32[2,128,32]{1,2,0:T(8,128)} async-done(((f32[2,128,128]{1,2,0:T(8,128)}), f32[2,128,32]{1,2,0:T(8,128)}) %reduce-scatter.4.cloned.1.call-update) | async-done | bytes 32784 | tf_op jit(solution)/shard_map/reduce_scatter | solution.py:24
  129.4 0.8 convert_element_type.63
  130.1 5.5 %fusion.6 = (f32[2,128]{1,0:T(2,128)S(1)}, f32[2,128,4096]{2,1,0:T(8,128)}, f32[2,128,4096]{2,1,0:T(8,128)S(1)}) fusion(f32[2,4096]{1,0:T(2,128)S(1)} %copy-done.6, f32[2,4096]{1,0:T(2,128)S(1)} %copy-done.8, pred[2,128]{1,0:T(4,128)(4,1)} %copy-done.11, bf16[2,64,4096]{2,1,0:T(8,128)(2,1)} %copy-done.2, bf16[2,64,4096]{2,1,0:T(8,128)(2,1)S(1)} %maximum_select_fusion.1, ...), kind=kOutput, calls=%fused_computation.9 | convolution fusion | flops 427065088 | bytes 13796609 | tf_op jit(solution)/shard_map/cth,cdh->ctd/dot_general | solution.py:124
  135.7 0.3 slice_select_fusion
  135.9 1.5 collective-permute-start.6
  137.5 43.5 %collective-permute-done.6 = f32[2,64,4096]{2,1,0:T(8,128)S(1)} collective-permute-done((f32[2,64,4096]{2,1,0:T(8,128)S(1)}, f32[2,64,4096]{2,1,0:T(8,128)S(1)}, u32[]{:S(2)}, u32[]{:S(2)}) %collective-permute-start.6) | collective-permute-done | bytes 2097184 | tf_op jit(solution)/shard_map/ppermute | solution.py:14
  181.0 0.4 select_add_fusion
  181.4 0.1 slice_select_fusion.1
  181.6 0.0 copy-start.14
  181.6 0.1 collective-permute-start.7
  181.7 2.6 %collective-permute-done.7 = f32[2,32,4096]{2,1,0:T(8,128)S(1)} collective-permute-done((f32[2,32,4096]{2,1,0:T(8,128)S(1)}, f32[2,32,4096]{2,1,0:T(8,128)S(1)}, u32[]{:S(2)}, u32[]{:S(2)}) %collective-permute-start.7) | collective-permute-done | bytes 1048608 | tf_op jit(solution)/shard_map/ppermute | solution.py:14
  184.3 1.2 select_add_fusion.1
  185.5 0.0 reduce-scatter.8.cloned.1.call-update
  185.6 0.1 broadcast_select_fusion.5
  185.6 1.5 collective-permute-start.8
  187.1 0.6 dynamic-slice.4
  187.7 1.6 collective-permute-done.8
  189.3 0.1 broadcast_select_fusion.3
  189.3 0.0 collective-permute-start.9
  189.4 0.1 fusion.50
  189.4 1.1 collective-permute-done.9
  190.5 0.1 select_add_fusion.2
  190.6 10.0 %all-reduce = f32[2,32,4]{1,0,2:T(2,128)S(1)} all-reduce(f32[2,32,4]{1,0,2:T(2,128)S(1)} %select_add_fusion.2), channel_id=6, replica_groups=mesh['section'=8,'tensor'=4] {'tensor'}, use_global_device_ids=true, to_apply=%region_8.9.clone | all-reduce | flops 256 | bytes 2048
  200.6 0.7 fusion.51
  201.2 10.7 %reduce-scatter.8.cloned.1.call-done = f32[2,32,1024]{2,1,0:T(8,128)} async-done(((f32[2,32,4096]{2,1,0:T(8,128)}), f32[2,32,1024]{2,1,0:T(8,128)}) %reduce-scatter.8.cloned.1.call-update) | async-done | bytes 262160 | tf_op jit(solution)/shard_map/reduce_scatter | solution.py:24
  212.0 1.2 fusion.32
  213.2 1.5 collective-permute-start.10
  214.8 3.5 %collective-permute-done.10 = bf16[2,32,1024]{2,1,0:T(8,128)(2,1)S(1)} collective-permute-done((bf16[2,32,1024]{2,1,0:T(8,128)(2,1)S(1)}, bf16[2,32,1024]{2,1,0:T(8,128)(2,1)S(1)}, u32[]{:S(2)}, u32[]{:S(2)}) %collective-permute-start.10) | collective-permute-done | bytes 131104 | tf_op jit(solution)/shard_map/ppermute | solution.py:19
  218.3 0.7 fusion.37
  (40 shorter events, 0.1 us)
Async XLA Ops:
  6.5 81.9 %copy-start = (bf16[1,2,128,128]{3,2,1,0:T(8,128)(2,1)S(1)}, bf16[1,2,128,128]{3,2,1,0:T(8,128)(2,1)}, u32[]{:S(2)}) copy-start(bf16[1,2,128,128]{3,2,1,0:T(8,128)(2,1)} %param.10) | copy-start | bytes 196612
  6.5 50.4 %copy-start.12 = (bf16[1,2,4096,32]{2,3,1,0:T(8,128)(2,1)S(1)}, bf16[1,2,4096,32]{2,3,1,0:T(8,128)(2,1)}, u32[]{:S(2)}) copy-start(bf16[1,2,4096,32]{2,3,1,0:T(8,128)(2,1)} %param.14) | copy-start | bytes 1572868
  6.5 102.9 %reduce-scatter.6.cloned.1.call-start = ((), (), s32[]{:S(2)}) async-start(), calls=%async_computation.4 | async-start | bytes 163840 | tf_op jit(solution)/shard_map/reduce_scatter | solution.py:25
  7.3 18.2 %collective-permute-start.2 = (bf16[2,32]{1,0:T(2,128)(2,1)S(1)}, bf16[2,32]{1,0:T(2,128)(2,1)S(1)}, u32[]{:S(2)}, u32[]{:S(2)}) collective-permute-start(bf16[2,32]{1,0:T(2,128)(2,1)S(1)} %convert_bitcast_fusion), channel_id=1, source_target_pairs={{0,4},{4,0},{8,12},{12,8},{16,20},{20,16},{24,28},{28,24},{1,5},{5... | collective-permute-start | bytes 392 | tf_op jit(solution)/shard_map/ppermute | solution.py:14
  7.8 19.3 %collective-permute-start.4 = (bf16[2,2,1024]{2,1,0:T(2,128)(2,1)}, bf16[2,2,1024]{2,1,0:T(2,128)(2,1)S(1)}, u32[]{:S(2)}, u32[]{:S(2)}) collective-permute-start(bf16[2,2,1024]{2,1,0:T(2,128)(2,1)} %bitcast.58), channel_id=1, source_target_pairs={{0,4},{4,0},{8,12},{12,8},{16,20},{20,16},{24,28},{28,24},{1,5},{5... | collective-permute-start | bytes 24584 | tf_op jit(solution)/shard_map/ppermute | solution.py:14
  25.5 6.3 %collective-permute-start = (bf16[2,32,4096]{2,1,0:T(8,128)(2,1)S(1)}, bf16[2,32,4096]{2,1,0:T(8,128)(2,1)S(1)}, u32[]{:S(2)}, u32[]{:S(2)}) collective-permute-start(bf16[2,32,4096]{2,1,0:T(8,128)(2,1)S(1)} %bitcast.52), channel_id=1, source_target_pairs={{0,4},{4,0},{8,12},{12,8},{16,20},{20,16},{24,28},{28,24},{1,5},{5... | collective-permute-start | bytes 1572872 | tf_op jit(solution)/shard_map/ppermute | solution.py:14
  25.6 3.6 %collective-permute-start.3 = (bf16[2,64]{1,0:T(2,128)(2,1)S(1)}, bf16[2,64]{1,0:T(2,128)(2,1)S(1)}, u32[]{:S(2)}, u32[]{:S(2)}) collective-permute-start(bf16[2,64]{1,0:T(2,128)(2,1)S(1)} %broadcast_select_fusion.6), channel_id=1, source_target_pairs={{0,8},{4,12},{8,0},{12,4},{16,24},{20,28},{24,16},{28,20},{1,9},{5... | collective-permute-start | bytes 776 | tf_op jit(solution)/shard_map/ppermute | solution.py:14
  27.9 3.8 %collective-permute-start.5 = (bf16[2,2,2048]{2,1,0:T(2,128)(2,1)S(1)}, bf16[2,2,2048]{2,1,0:T(2,128)(2,1)S(1)}, u32[]{:S(2)}, u32[]{:S(2)}) collective-permute-start(bf16[2,2,2048]{2,1,0:T(2,128)(2,1)S(1)} %broadcast_select_fusion.2), channel_id=1, source_target_pairs={{0,8},{4,12},{8,0},{12,4},{16,24},{20,28},{24,16},{28,20},{1,9},{5... | collective-permute-start | bytes 49160 | tf_op jit(solution)/shard_map/ppermute | solution.py:14
  29.2 56.9 %copy-start.11 = (pred[2,128]{1,0:T(4,128)(4,1)}, pred[2,128]{1,0:T(4,128)(4,1)S(1)}, u32[]{:S(2)}) copy-start(pred[2,128]{1,0:T(4,128)(4,1)S(1)} %fusion.52) | copy-start | bytes 772
  32.0 24.2 %collective-permute-start.1 = (bf16[2,64,4096]{2,1,0:T(8,128)(2,1)S(1)}, bf16[2,64,4096]{2,1,0:T(8,128)(2,1)S(1)}, u32[]{:S(2)}, u32[]{:S(2)}) collective-permute-start(bf16[2,64,4096]{2,1,0:T(8,128)(2,1)S(1)} %maximum_select_fusion.1), channel_id=1, source_target_pairs={{0,8},{4,12},{8,0},{12,4},{16,24},{20,28},{24,16},{28,20},{1,9},{5... | collective-permute-start | bytes 3145736 | tf_op jit(solution)/shard_map/ppermute | solution.py:14
  32.7 53.5 %copy-start.5 = (f32[2,4096]{1,0:T(2,128)}, f32[2,4096]{1,0:T(2,128)S(1)}, u32[]{:S(2)}) copy-start(f32[2,4096]{1,0:T(2,128)S(1)} %get-tuple-element.16) | copy-start | bytes 98308
  32.7 53.5 %copy-start.7 = (f32[2,4096]{1,0:T(2,128)}, f32[2,4096]{1,0:T(2,128)S(1)}, u32[]{:S(2)}) copy-start(f32[2,4096]{1,0:T(2,128)S(1)} %get-tuple-element.17) | copy-start | bytes 98308
  56.2 30.0 %copy-start.2 = (bf16[2,64,4096]{2,1,0:T(8,128)(2,1)}, bf16[2,64,4096]{2,1,0:T(8,128)(2,1)S(1)}, u32[]{:S(2)}) copy-start(bf16[2,64,4096]{2,1,0:T(8,128)(2,1)S(1)} %collective-permute-done.1) | copy-start | bytes 3145732
  56.9 29.2 %copy-start.9 = (f32[2,128]{1,0:T(2,128)}, f32[2,128]{1,0:T(2,128)S(1)}, u32[]{:S(2)}) copy-start(f32[2,128]{1,0:T(2,128)S(1)} %add_rsqrt_fusion) | copy-start | bytes 3076
  56.9 14.7 %copy-start.13 = (bf16[1,2,4096,32]{2,3,1,0:T(8,128)(2,1)S(1)}, bf16[1,2,4096,32]{2,3,1,0:T(8,128)(2,1)}, u32[]{:S(2)}) copy-start(bf16[1,2,4096,32]{2,3,1,0:T(8,128)(2,1)} %param.15) | copy-start | bytes 1572868
  71.7 14.5 %copy-start.1 = (bf16[1,2,4096,128]{3,2,1,0:T(8,128)(2,1)S(1)}, bf16[1,2,4096,128]{3,2,1,0:T(8,128)(2,1)}, u32[]{:S(2)}) copy-start(bf16[1,2,4096,128]{3,2,1,0:T(8,128)(2,1)} %param.13) | copy-start | bytes 6291460
  89.4 40.0 %reduce-scatter.4.cloned.1.call-start = ((), (), s32[]{:S(2)}) async-start(), calls=%async_computation.3 | async-start | bytes 163840 | tf_op jit(solution)/shard_map/reduce_scatter | solution.py:24
  89.6 40.5 %copy-start.6 = (f32[2,4096]{1,0:T(2,128)S(1)}, f32[2,4096]{1,0:T(2,128)}, u32[]{:S(2)}) copy-start(f32[2,4096]{1,0:T(2,128)} %copy-done.5) | copy-start | bytes 98308
  89.6 40.5 %copy-start.8 = (f32[2,4096]{1,0:T(2,128)S(1)}, f32[2,4096]{1,0:T(2,128)}, u32[]{:S(2)}) copy-start(f32[2,4096]{1,0:T(2,128)} %copy-done.7) | copy-start | bytes 98308
  91.5 120.5 %reduce-scatter.8.cloned.1.call-start = ((), (), s32[]{:S(2)}) async-start(), calls=%async_computation.5 | async-start | bytes 1310720 | tf_op jit(solution)/shard_map/reduce_scatter | solution.py:24
  135.9 45.1 %collective-permute-start.6 = (f32[2,64,4096]{2,1,0:T(8,128)S(1)}, f32[2,64,4096]{2,1,0:T(8,128)S(1)}, u32[]{:S(2)}, u32[]{:S(2)}) collective-permute-start(f32[2,64,4096]{2,1,0:T(8,128)S(1)} %slice_select_fusion), channel_id=1, source_target_pairs={{0,8},{4,12},{8,0},{12,4},{16,24},{20,28},{24,16},{28,20},{1,9},{5... | collective-permute-start | bytes 6291464 | tf_op jit(solution)/shard_map/ppermute | solution.py:14
  181.6 5.5 %copy-start.14 = (u32[32]{0:T(128)S(1)}, u32[32]{0:T(128)}, u32[]{:S(2)}) copy-start(u32[32]{0:T(128)} %constant.90) | copy-start | bytes 388
  181.6 7.8 %copy-start.10 = (f32[2,128]{1,0:T(2,128)S(1)}, f32[2,128]{1,0:T(2,128)}, u32[]{:S(2)}) copy-start(f32[2,128]{1,0:T(2,128)} %copy-done.9) | copy-start | bytes 3076
  181.6 30.4 %copy-start.3 = (bf16[1,2,32,1024]{3,2,1,0:T(8,128)(2,1)S(1)}, bf16[1,2,32,1024]{3,2,1,0:T(8,128)(2,1)}, u32[]{:S(2)}) copy-start(bf16[1,2,32,1024]{3,2,1,0:T(8,128)(2,1)} %param.8) | copy-start | bytes 393220
  181.6 30.4 %copy-start.4 = (bf16[1,2,32,1024]{3,2,1,0:T(8,128)(2,1)S(1)}, bf16[1,2,32,1024]{3,2,1,0:T(8,128)(2,1)}, u32[]{:S(2)}) copy-start(bf16[1,2,32,1024]{3,2,1,0:T(8,128)(2,1)} %param.9) | copy-start | bytes 393220
  181.6 2.7 %collective-permute-start.7 = (f32[2,32,4096]{2,1,0:T(8,128)S(1)}, f32[2,32,4096]{2,1,0:T(8,128)S(1)}, u32[]{:S(2)}, u32[]{:S(2)}) collective-permute-start(f32[2,32,4096]{2,1,0:T(8,128)S(1)} %slice_select_fusion.1), channel_id=1, source_target_pairs={{0,4},{4,0},{8,12},{12,8},{16,20},{20,16},{24,28},{28,24},{1,5},{5... | collective-permute-start | bytes 3145736 | tf_op jit(solution)/shard_map/ppermute | solution.py:14
  185.6 3.6 %collective-permute-start.8 = (f32[2,64,4]{1,0,2:T(2,128)S(1)}, f32[2,64,4]{1,0,2:T(2,128)S(1)}, u32[]{:S(2)}, u32[]{:S(2)}) collective-permute-start(f32[2,64,4]{1,0,2:T(2,128)S(1)} %broadcast_in_dim.67), channel_id=1, source_target_pairs={{0,8},{4,12},{8,0},{12,4},{16,24},{20,28},{24,16},{28,20},{1,9},{5... | collective-permute-start | bytes 6152 | tf_op jit(solution)/shard_map/ppermute | solution.py:14
  189.3 1.2 collective-permute-start.9
  213.2 5.0 %collective-permute-start.10 = (bf16[2,32,1024]{2,1,0:T(8,128)(2,1)S(1)}, bf16[2,32,1024]{2,1,0:T(8,128)(2,1)S(1)}, u32[]{:S(2)}, u32[]{:S(2)}) collective-permute-start(bf16[2,32,1024]{2,1,0:T(8,128)(2,1)S(1)} %fusion.32), channel_id=1, source_target_pairs={{0,16},{4,20},{8,24},{12,28},{16,0},{20,4},{24,8},{28,12},{1,17},{... | collective-permute-start | bytes 393224 | tf_op jit(solution)/shard_map/ppermute | solution.py:19
Sparse Core Ops, SparseCore 0:
  89.5 19.9 reduce-scatter.5
  111.7 17.5 reduce-scatter.3
  185.7 26.2 reduce-scatter.7
where the time goes:
time: 226 us; the launch traced here: 225 us
  waiting for transfers between devices  123 us (54%)
  blocking collectives  54.3 us (24%)
  matrix products  13.8 us (6%)
  between operations  13.4 us (6%)
  other arithmetic  9.83 us (4%)
  starting transfers between devices  7.91 us (4%)
  local copies, waits for them, and re-layouts  3.58 us (2%)
    ppermute x10, waiting for transfers between devices, swapped(): return lax.ppermute(value, axis, pairs)  75.4 us
    reduce_scatter x2, waiting for transfers between devices, sum_columns(): lax.psum_scatter(first, 'tensor', scatter_dimension=2, tiled=True)  29.9 us
    all_gather x1, blocking collectives, per_device(): x_cols = lax.all_gather(x_local, 'tensor', axis=2, tiled=True)  17.7 us
    reduce_scatter x1, waiting for transfers between devices, sum_columns(): lax.psum_scatter(second, 'tensor', scatter_dimension=2, tiled=True)  13.9 us
    all_gather x1, blocking collectives, per_device(): lax.all_gather(key_part, 'tensor', axis=2, tiled=True)  13.4 us
    all_gather x1, blocking collectives, per_device(): lax.all_gather(value_part, 'tensor', axis=2, tiled=True)  13.2 us
    unnamed x1, blocking collectives  10 us
    ppermute x10, starting transfers between devices, swapped(): return lax.ppermute(value, axis, pairs)  6.29 us
  transfers between devices with their start and end apart: 14, of which 11 were waited for; matrix products, arithmetic and copies ran while one was open for 4% of the time, Pallas kernels for 0%

commit v1 on v0

--- a/solution.py
+++ b/solution.py
@@ -6,6 +6,18 @@
 HEAD_DIM = 128
 SUB = 4
 epsilon = 1e-05
+
+
+def doubled_up(value, axis, dim):
+    ways, here, step = (lax.axis_size(axis), lax.axis_index(axis), value.shape[dim])
+    line, have = (value, 1)
+    while have < ways:
+        line = jnp.concatenate(
+            [line, lax.ppermute(line, axis, [(d, (d - have) % ways) for d in range(ways)])],
+            axis=dim,
+        )
+        have = 2 * have
+    return jnp.roll(line, here * step, axis=dim)
 
 
 def swapped(value, axis, stride):
@@ -90,7 +102,7 @@
     ).astype(jnp.bfloat16)
     key_rows, value_rows = (
         lax.all_gather(key_part, "tensor", axis=2, tiled=True),
-        lax.all_gather(value_part, "tensor", axis=2, tiled=True),
+        doubled_up(value_part, "tensor", 2),
     )
     softmax_scale = HEAD_DIM ** (-0.5)
     scores = (

time: 226 us -> 215 us (0.951)
  blocking collectives: 54.3 us -> 41.1 us
  waiting for transfers between devices: 123 us -> 114 us
  starting transfers between devices: 7.91 us -> 12.6 us
  local copies, waits for them, and re-layouts: 3.58 us -> 7.93 us
    all_gather x1 -> x0, blocking collectives: 13.2 us -> none  [per_device(): lax.all_gather(value_part, 'tensor', axis=2, tiled=True)]
    reduce_scatter x1, waiting for transfers between devices: 13.9 us -> 2.23 us  [sum_columns(): lax.psum_scatter(second, 'tensor', scatter_dimension=2, tiled=True)]
    ppermute x0 -> x2, starting transfers between devices: none -> 4.74 us  [doubled_up(): lax.ppermute(line, axis, [(d, (d - have) % ways) for d in range(ways)])]
    unnamed x34 -> x40, local copies, waits for them, and re-layouts: 3.52 us -> 7.26 us
    ppermute x0 -> x2, waiting for transfers between devices: none -> 3.32 us  [doubled_up(): lax.ppermute(line, axis, [(d, (d - have) % ways) for d in range(ways)])]
  transfers between devices with their start and end apart: 14 -> 16, of which waited for: 11 -> 12; matrix products, arithmetic and copies ran while one was open for 4% -> 7% of each run, Pallas kernels for 0% -> 0%
where the time goes in v1:
time: 215 us
  waiting for transfers between devices  114 us (53%)
  blocking collectives  41.1 us (19%)
  matrix products  14.7 us (7%)
  between operations  13.4 us (6%)
  starting transfers between devices  12.6 us (6%)
  other arithmetic  10.5 us (5%)
  local copies, waits for them, and re-layouts  7.93 us (4%)
    ppermute x10, waiting for transfers between devices, swapped(): return lax.ppermute(value, axis, pairs)  75.4 us
    reduce_scatter x2, waiting for transfers between devices, sum_columns(): lax.psum_scatter(first, 'tensor', scatter_dimension=2, tiled=True)  30 us
    all_gather x1, blocking collectives, per_device(): x_cols = lax.all_gather(x_local, 'tensor', axis=2, tiled=True)  17.7 us
    all_gather x1, blocking collectives, per_device(): lax.all_gather(key_part, 'tensor', axis=2, tiled=True)  13.4 us
    unnamed x1, blocking collectives  10 us
    unnamed x40, local copies, waits for them, and re-layouts  7.26 us
    ppermute x10, starting transfers between devices, swapped(): return lax.ppermute(value, axis, pairs)  6.3 us
    dot_general x1, matrix products, per_device(): jnp.einsum('cth,cdh->ctd', joined_grads, joined_weights, preferred_elemen...  5.48 us
  transfers between devices with their start and end apart: 16, of which 12 were waited for; matrix products, arithmetic and copies ran while one was open for 7% of the time, Pallas kernels for 0%

profile of v1, /device:TPU:0, one launch (start us, length us, event | category | flops | bytes accessed | tf_op | source)
XLA Modules:
  0.0 214.8 jit_solution(2440480266309203986)
XLA Ops:
  6.5 0.7 convert_bitcast_fusion
  7.3 0.5 collective-permute-start.2
  7.8 17.7 %all-gather = bf16[1,2,32,4096]{3,2,1,0:T(8,128)(2,1)S(1)} all-gather(bf16[1,2,32,1024]{3,2,1,0:T(8,128)(2,1)} %param.8), channel_id=2, replica_groups=mesh['section'=8,'tensor'=4] {'tensor'}, dimensions={3}, use_global_device_ids=true | all-gather | bytes 655360 | tf_op jit(solution)/shard_map/all_gather | solution.py:82
  25.5 0.1 broadcast_select_fusion.6
  25.6 1.5 collective-permute-start.3
  27.1 0.8 broadcast_select_fusion.2
  27.9 0.6 collective-permute-start.5
  28.5 0.7 collective-permute-done.3
  29.2 0.1 fusion.54
  29.2 2.4 %collective-permute-done.5 = bf16[2,2,2048]{2,1,0:T(2,128)(2,1)S(1)} collective-permute-done((bf16[2,2,2048]{2,1,0:T(2,128)(2,1)S(1)}, bf16[2,2,2048]{2,1,0:T(2,128)(2,1)S(1)}, u32[]{:S(2)}, u32[]{:S(2)}) %collective-permute-start.5) | collective-permute-done | bytes 16416 | tf_op jit(solution)/shard_map/ppermute | solution.py:26
  31.7 0.2 maximum_select_fusion.1
  31.9 0.6 collective-permute-start.1
  32.6 0.1 copy_bitcast_fusion
  32.7 23.5 %collective-permute-done.1 = bf16[2,64,4096]{2,1,0:T(8,128)(2,1)S(1)} collective-permute-done((bf16[2,64,4096]{2,1,0:T(8,128)(2,1)S(1)}, bf16[2,64,4096]{2,1,0:T(8,128)(2,1)S(1)}, u32[]{:S(2)}, u32[]{:S(2)}) %collective-permute-start.1) | collective-permute-done | bytes 1048608 | tf_op jit(solution)/shard_map/ppermute | solution.py:26
  56.2 0.8 fusion.2
  57.0 1.3 convolution_convert_fusion.2
  58.2 13.4 %all_gather.7 = bf16[2,128,128]{1,2,0:T(8,128)(2,1)S(1)} all-gather(bf16[2,128,32]{1,2,0:T(8,128)(2,1)S(1)} %convolution_convert_fusion.2), channel_id=1, replica_groups=mesh['section'=8,'tensor'=4] {'tensor'}, dimensions={2}, use_global_device_ids=true | all-gather | bytes 81920 | tf_op jit(solution)/shard_map/all_gather | solution.py:104
  71.7 1.4 fusion.22
  73.0 0.6 copy-done.5
  73.6 0.2 fusion.18
  73.9 0.7 fusion.63
  74.6 1.9 constant_dynamic-update-slice_fusion.5
  76.5 3.8 %collective-permute-start.6 = (bf16[2,128,32]{1,2,0:T(8,128)(2,1)}, bf16[2,128,32]{1,2,0:T(8,128)(2,1)S(1)}, u32[]{:S(2)}, u32[]{:S(2)}) collective-permute-start(bf16[2,128,32]{1,2,0:T(8,128)(2,1)} %get-tuple-element.16), channel_id=1, source_target_pairs={{0,3},{1,0},{2,1},{3,2},{4,7},{5,4},{6,5},{7,6},{8,11},{9,8},{10,9... | collective-permute-start | bytes 49160 | tf_op jit(solution)/shard_map/ppermute | solution.py:16
  80.3 1.5 fusion.43
  82.0 0.7 pad_maximum_fusion
  82.7 0.9 collective-permute-start.7
  83.6 0.6 constant_dynamic-update-slice_fusion.4
  84.2 3.3 %collective-permute-done.7 = bf16[2,128,64]{1,2,0:T(8,128)(2,1)S(1)} collective-permute-done((bf16[2,128,64]{1,2,0:T(8,128)(2,1)S(1)}, bf16[2,128,64]{1,2,0:T(8,128)(2,1)S(1)}, u32[]{:S(2)}, u32[]{:S(2)}) %collective-permute-start.7) | collective-permute-done | bytes 32800 | tf_op jit(solution)/shard_map/ppermute | solution.py:16
  87.5 0.6 constant_dynamic-update-slice_fusion.3
  88.1 1.3 constant_dynamic-update-slice_fusion.2
  89.5 0.6 constant_dynamic-update-slice_fusion.1
  90.1 0.6 constant_dynamic-update-slice_fusion
  90.7 1.0 convolution_bitcast_fusion
  91.7 1.7 fusion.25
  93.6 2.8 %copy.12 = bf16[1,2,4096,128]{2,3,1,0:T(8,128)(2,1)} copy(bf16[1,2,4096,128]{3,2,1,0:T(8,128)(2,1)S(1)} %copy-done.1) | data formatting | bytes 4194304 | tf_op args[5]
  96.4 0.2 convolution_convert_fusion
  96.5 2.2 %reduce-scatter.6.cloned.1.call-done = f32[2,128,32]{1,2,0:T(8,128)} async-done(((f32[2,128,128]{1,2,0:T(8,128)}), f32[2,128,32]{1,2,0:T(8,128)}) %reduce-scatter.6.cloned.1.call-update) | async-done | bytes 32784 | tf_op jit(solution)/shard_map/reduce_scatter | solution.py:37
  98.8 0.8 convert_element_type.65
  99.5 19.1 %reduce-scatter.4.cloned.1.call-done = f32[2,128,32]{1,2,0:T(8,128)} async-done(((f32[2,128,128]{1,2,0:T(8,128)}), f32[2,128,32]{1,2,0:T(8,128)}) %reduce-scatter.4.cloned.1.call-update) | async-done | bytes 32784 | tf_op jit(solution)/shard_map/reduce_scatter | solution.py:36
  118.7 0.8 convert_element_type.63
  119.4 5.5 %fusion.6 = (f32[2,128]{1,0:T(2,128)S(1)}, f32[2,128,4096]{2,1,0:T(8,128)}, f32[2,128,4096]{2,1,0:T(8,128)S(1)}) fusion(f32[2,4096]{1,0:T(2,128)} %copy-done.6, f32[2,4096]{1,0:T(2,128)} %copy-done.7, pred[2,128]{1,0:T(4,128)(4,1)S(1)} %copy-done.12, bf16[2,64,4096]{2,1,0:T(8,128)(2,1)} %copy-done.2, bf16[2,64,4096]{2,1,0:T(8,128)(2,1)S(1)} %maximum_select_fusion.1, ...), kind=kOutput, calls=%fused_computation.9 | convolution fusion | flops 427065088 | bytes 13796609 | tf_op jit(solution)/shard_map/cth,cdh->ctd/dot_general | solution.py:136
  124.9 0.3 slice_select_fusion
  125.2 1.5 collective-permute-start.8
  126.7 43.5 %collective-permute-done.8 = f32[2,64,4096]{2,1,0:T(8,128)S(1)} collective-permute-done((f32[2,64,4096]{2,1,0:T(8,128)S(1)}, f32[2,64,4096]{2,1,0:T(8,128)S(1)}, u32[]{:S(2)}, u32[]{:S(2)}) %collective-permute-start.8) | collective-permute-done | bytes 2097184 | tf_op jit(solution)/shard_map/ppermute | solution.py:26
  170.3 0.4 select_add_fusion
  170.7 0.1 slice_select_fusion.1
  170.9 0.1 collective-permute-start.9
  170.9 2.6 %collective-permute-done.9 = f32[2,32,4096]{2,1,0:T(8,128)S(1)} collective-permute-done((f32[2,32,4096]{2,1,0:T(8,128)S(1)}, f32[2,32,4096]{2,1,0:T(8,128)S(1)}, u32[]{:S(2)}, u32[]{:S(2)}) %collective-permute-start.9) | collective-permute-done | bytes 1048608 | tf_op jit(solution)/shard_map/ppermute | solution.py:26
  173.6 1.2 select_add_fusion.1
  174.8 0.1 broadcast_select_fusion.5
  174.9 1.5 collective-permute-start.10
  176.4 0.6 dynamic-slice.4
  177.0 1.5 collective-permute-done.10
  178.5 0.1 broadcast_select_fusion.3
  178.6 0.1 fusion.51
  178.7 1.1 collective-permute-done.11
  179.8 0.1 select_add_fusion.2
  179.8 10.0 %all-reduce = f32[2,32,4]{1,0,2:T(2,128)S(1)} all-reduce(f32[2,32,4]{1,0,2:T(2,128)S(1)} %select_add_fusion.2), channel_id=6, replica_groups=mesh['section'=8,'tensor'=4] {'tensor'}, use_global_device_ids=true, to_apply=%region_8.9.clone | all-reduce | flops 256 | bytes 2048
  189.9 0.7 fusion.52
  190.5 10.8 %reduce-scatter.8.cloned.1.call-done = f32[2,32,1024]{2,1,0:T(8,128)} async-done(((f32[2,32,4096]{2,1,0:T(8,128)}), f32[2,32,1024]{2,1,0:T(8,128)}) %reduce-scatter.8.cloned.1.call-update) | async-done | bytes 262160 | tf_op jit(solution)/shard_map/reduce_scatter | solution.py:36
  201.4 1.2 fusion.32
  202.6 1.5 collective-permute-start.12
  204.1 3.5 %collective-permute-done.12 = bf16[2,32,1024]{2,1,0:T(8,128)(2,1)S(1)} collective-permute-done((bf16[2,32,1024]{2,1,0:T(8,128)(2,1)S(1)}, bf16[2,32,1024]{2,1,0:T(8,128)(2,1)S(1)}, u32[]{:S(2)}, u32[]{:S(2)}) %collective-permute-start.12) | collective-permute-done | bytes 131104 | tf_op jit(solution)/shard_map/ppermute | solution.py:31
  207.6 0.7 fusion.37
  (51 shorter events, 0.4 us)
Async XLA Ops:
  6.5 73.8 %copy-start = (bf16[1,2,128,128]{3,2,1,0:T(8,128)(2,1)S(1)}, bf16[1,2,128,128]{3,2,1,0:T(8,128)(2,1)}, u32[]{:S(2)}) copy-start(bf16[1,2,128,128]{3,2,1,0:T(8,128)(2,1)} %param.10) | copy-start | bytes 196612
  6.5 92.2 %reduce-scatter.6.cloned.1.call-start = ((), (), s32[]{:S(2)}) async-start(), calls=%async_computation.4 | async-start | bytes 163840 | tf_op jit(solution)/shard_map/reduce_scatter | solution.py:37
  7.3 18.2 %collective-permute-start.2 = (bf16[2,32]{1,0:T(2,128)(2,1)S(1)}, bf16[2,32]{1,0:T(2,128)(2,1)S(1)}, u32[]{:S(2)}, u32[]{:S(2)}) collective-permute-start(bf16[2,32]{1,0:T(2,128)(2,1)S(1)} %convert_bitcast_fusion), channel_id=1, source_target_pairs={{0,4},{4,0},{8,12},{12,8},{16,20},{20,16},{24,28},{28,24},{1,5},{5... | collective-permute-start | bytes 392 | tf_op jit(solution)/shard_map/ppermute | solution.py:26
  7.7 19.3 %collective-permute-start.4 = (bf16[2,2,1024]{2,1,0:T(2,128)(2,1)}, bf16[2,2,1024]{2,1,0:T(2,128)(2,1)S(1)}, u32[]{:S(2)}, u32[]{:S(2)}) collective-permute-start(bf16[2,2,1024]{2,1,0:T(2,128)(2,1)} %bitcast.59), channel_id=1, source_target_pairs={{0,4},{4,0},{8,12},{12,8},{16,20},{20,16},{24,28},{28,24},{1,5},{5... | collective-permute-start | bytes 24584 | tf_op jit(solution)/shard_map/ppermute | solution.py:26
  25.4 6.3 %collective-permute-start = (bf16[2,32,4096]{2,1,0:T(8,128)(2,1)S(1)}, bf16[2,32,4096]{2,1,0:T(8,128)(2,1)S(1)}, u32[]{:S(2)}, u32[]{:S(2)}) collective-permute-start(bf16[2,32,4096]{2,1,0:T(8,128)(2,1)S(1)} %bitcast.53), channel_id=1, source_target_pairs={{0,4},{4,0},{8,12},{12,8},{16,20},{20,16},{24,28},{28,24},{1,5},{5... | collective-permute-start | bytes 1572872 | tf_op jit(solution)/shard_map/ppermute | solution.py:26
  25.5 31.5 %copy-start.13 = (bf16[1,2,4096,32]{2,3,1,0:T(8,128)(2,1)S(1)}, bf16[1,2,4096,32]{2,3,1,0:T(8,128)(2,1)}, u32[]{:S(2)}) copy-start(bf16[1,2,4096,32]{2,3,1,0:T(8,128)(2,1)} %param.14) | copy-start | bytes 1572868
  25.6 3.6 %collective-permute-start.3 = (bf16[2,64]{1,0:T(2,128)(2,1)S(1)}, bf16[2,64]{1,0:T(2,128)(2,1)S(1)}, u32[]{:S(2)}, u32[]{:S(2)}) collective-permute-start(bf16[2,64]{1,0:T(2,128)(2,1)S(1)} %broadcast_select_fusion.6), channel_id=1, source_target_pairs={{0,8},{4,12},{8,0},{12,4},{16,24},{20,28},{24,16},{28,20},{1,9},{5... | collective-permute-start | bytes 776 | tf_op jit(solution)/shard_map/ppermute | solution.py:26
  27.9 3.8 %collective-permute-start.5 = (bf16[2,2,2048]{2,1,0:T(2,128)(2,1)S(1)}, bf16[2,2,2048]{2,1,0:T(2,128)(2,1)S(1)}, u32[]{:S(2)}, u32[]{:S(2)}) collective-permute-start(bf16[2,2,2048]{2,1,0:T(2,128)(2,1)S(1)} %broadcast_select_fusion.2), channel_id=1, source_target_pairs={{0,8},{4,12},{8,0},{12,4},{16,24},{20,28},{24,16},{28,20},{1,9},{5... | collective-permute-start | bytes 49160 | tf_op jit(solution)/shard_map/ppermute | solution.py:26
  29.2 45.4 %copy-start.11 = (pred[2,128]{1,0:T(4,128)(4,1)}, pred[2,128]{1,0:T(4,128)(4,1)S(1)}, u32[]{:S(2)}) copy-start(pred[2,128]{1,0:T(4,128)(4,1)S(1)} %fusion.54) | copy-start | bytes 772
  31.9 24.2 %collective-permute-start.1 = (bf16[2,64,4096]{2,1,0:T(8,128)(2,1)S(1)}, bf16[2,64,4096]{2,1,0:T(8,128)(2,1)S(1)}, u32[]{:S(2)}, u32[]{:S(2)}) collective-permute-start(bf16[2,64,4096]{2,1,0:T(8,128)(2,1)S(1)} %maximum_select_fusion.1), channel_id=1, source_target_pairs={{0,8},{4,12},{8,0},{12,4},{16,24},{20,28},{24,16},{28,20},{1,9},{5... | collective-permute-start | bytes 3145736 | tf_op jit(solution)/shard_map/ppermute | solution.py:26
  32.7 41.9 %copy-start.6 = (f32[2,4096]{1,0:T(2,128)}, f32[2,4096]{1,0:T(2,128)S(1)}, u32[]{:S(2)}) copy-start(f32[2,4096]{1,0:T(2,128)S(1)} %get-tuple-element.18) | copy-start | bytes 98308
  32.7 41.9 %copy-start.7 = (f32[2,4096]{1,0:T(2,128)}, f32[2,4096]{1,0:T(2,128)S(1)}, u32[]{:S(2)}) copy-start(f32[2,4096]{1,0:T(2,128)S(1)} %get-tuple-element.19) | copy-start | bytes 98308
  56.2 18.4 %copy-start.2 = (bf16[2,64,4096]{2,1,0:T(8,128)(2,1)}, bf16[2,64,4096]{2,1,0:T(8,128)(2,1)S(1)}, u32[]{:S(2)}) copy-start(bf16[2,64,4096]{2,1,0:T(8,128)(2,1)S(1)} %collective-permute-done.1) | copy-start | bytes 3145732
  56.9 17.7 %copy-start.8 = (f32[2,128]{1,0:T(2,128)}, f32[2,128]{1,0:T(2,128)S(1)}, u32[]{:S(2)}) copy-start(f32[2,128]{1,0:T(2,128)S(1)} %add_rsqrt_fusion) | copy-start | bytes 3076
  56.9 14.7 %copy-start.1 = (bf16[1,2,4096,128]{3,2,1,0:T(8,128)(2,1)S(1)}, bf16[1,2,4096,128]{3,2,1,0:T(8,128)(2,1)}, u32[]{:S(2)}) copy-start(bf16[1,2,4096,128]{3,2,1,0:T(8,128)(2,1)} %param.13) | copy-start | bytes 6291460
  71.7 2.9 %copy-start.14 = (bf16[1,2,4096,32]{2,3,1,0:T(8,128)(2,1)S(1)}, bf16[1,2,4096,32]{2,3,1,0:T(8,128)(2,1)}, u32[]{:S(2)}) copy-start(bf16[1,2,4096,32]{2,3,1,0:T(8,128)(2,1)} %param.15) | copy-start | bytes 1572868
  73.0 0.6 copy-start.5
  76.5 5.5 %collective-permute-start.6 = (bf16[2,128,32]{1,2,0:T(8,128)(2,1)}, bf16[2,128,32]{1,2,0:T(8,128)(2,1)S(1)}, u32[]{:S(2)}, u32[]{:S(2)}) collective-permute-start(bf16[2,128,32]{1,2,0:T(8,128)(2,1)} %get-tuple-element.16), channel_id=1, source_target_pairs={{0,3},{1,0},{2,1},{3,2},{4,7},{5,4},{6,5},{7,6},{8,11},{9,8},{10,9... | collective-permute-start | bytes 49160 | tf_op jit(solution)/shard_map/ppermute | solution.py:16
  81.9 14.5 %copy-start.10 = (f32[2,128]{1,0:T(2,128)S(1)}, f32[2,128]{1,0:T(2,128)}, u32[]{:S(2)}) copy-start(f32[2,128]{1,0:T(2,128)} %get-tuple-element.13) | copy-start | bytes 3076
  81.9 37.6 %copy-start.12 = (pred[2,128]{1,0:T(4,128)(4,1)S(1)}, pred[2,128]{1,0:T(4,128)(4,1)}, u32[]{:S(2)}) copy-start(pred[2,128]{1,0:T(4,128)(4,1)} %copy-done.11) | copy-start | bytes 772
  81.9 36.8 %reduce-scatter.4.cloned.1.call-start = ((), (), s32[]{:S(2)}) async-start(), calls=%async_computation.3 | async-start | bytes 163840 | tf_op jit(solution)/shard_map/reduce_scatter | solution.py:36
  82.7 4.8 %collective-permute-start.7 = (bf16[2,128,64]{1,2,0:T(8,128)(2,1)S(1)}, bf16[2,128,64]{1,2,0:T(8,128)(2,1)S(1)}, u32[]{:S(2)}, u32[]{:S(2)}) collective-permute-start(bf16[2,128,64]{1,2,0:T(8,128)(2,1)S(1)} %pad_maximum_fusion), channel_id=1, source_target_pairs={{0,2},{1,3},{2,0},{3,1},{4,6},{5,7},{6,4},{7,5},{8,10},{9,11},{10,... | collective-permute-start | bytes 98312 | tf_op jit(solution)/shard_map/ppermute | solution.py:16
  93.5 107.9 %reduce-scatter.8.cloned.1.call-start = ((), (), s32[]{:S(2)}) async-start(), calls=%async_computation.5 | async-start | bytes 1310720 | tf_op jit(solution)/shard_map/reduce_scatter | solution.py:36
  125.2 45.1 %collective-permute-start.8 = (f32[2,64,4096]{2,1,0:T(8,128)S(1)}, f32[2,64,4096]{2,1,0:T(8,128)S(1)}, u32[]{:S(2)}, u32[]{:S(2)}) collective-permute-start(f32[2,64,4096]{2,1,0:T(8,128)S(1)} %slice_select_fusion), channel_id=1, source_target_pairs={{0,8},{4,12},{8,0},{12,4},{16,24},{20,28},{24,16},{28,20},{1,9},{5... | collective-permute-start | bytes 6291464 | tf_op jit(solution)/shard_map/ppermute | solution.py:26
  170.8 5.6 %copy-start.15 = (u32[32]{0:T(128)S(1)}, u32[32]{0:T(128)}, u32[]{:S(2)}) copy-start(u32[32]{0:T(128)} %constant.110) | copy-start | bytes 388
  170.8 7.8 %copy-start.9 = (f32[2,128]{1,0:T(2,128)S(1)}, f32[2,128]{1,0:T(2,128)}, u32[]{:S(2)}) copy-start(f32[2,128]{1,0:T(2,128)} %copy-done.8) | copy-start | bytes 3076
  170.8 30.5 %copy-start.3 = (bf16[1,2,32,1024]{3,2,1,0:T(8,128)(2,1)S(1)}, bf16[1,2,32,1024]{3,2,1,0:T(8,128)(2,1)}, u32[]{:S(2)}) copy-start(bf16[1,2,32,1024]{3,2,1,0:T(8,128)(2,1)} %param.8) | copy-start | bytes 393220
  170.9 30.5 %copy-start.4 = (bf16[1,2,32,1024]{3,2,1,0:T(8,128)(2,1)S(1)}, bf16[1,2,32,1024]{3,2,1,0:T(8,128)(2,1)}, u32[]{:S(2)}) copy-start(bf16[1,2,32,1024]{3,2,1,0:T(8,128)(2,1)} %param.9) | copy-start | bytes 393220
  170.9 2.7 %collective-permute-start.9 = (f32[2,32,4096]{2,1,0:T(8,128)S(1)}, f32[2,32,4096]{2,1,0:T(8,128)S(1)}, u32[]{:S(2)}, u32[]{:S(2)}) collective-permute-start(f32[2,32,4096]{2,1,0:T(8,128)S(1)} %slice_select_fusion.1), channel_id=1, source_target_pairs={{0,4},{4,0},{8,12},{12,8},{16,20},{20,16},{24,28},{28,24},{1,5},{5... | collective-permute-start | bytes 3145736 | tf_op jit(solution)/shard_map/ppermute | solution.py:26
  174.9 3.6 %collective-permute-start.10 = (f32[2,64,4]{1,0,2:T(2,128)S(1)}, f32[2,64,4]{1,0,2:T(2,128)S(1)}, u32[]{:S(2)}, u32[]{:S(2)}) collective-permute-start(f32[2,64,4]{1,0,2:T(2,128)S(1)} %broadcast_in_dim.67), channel_id=1, source_target_pairs={{0,8},{4,12},{8,0},{12,4},{16,24},{20,28},{24,16},{28,20},{1,9},{5... | collective-permute-start | bytes 6152 | tf_op jit(solution)/shard_map/ppermute | solution.py:26
  178.6 1.2 collective-permute-start.11
  202.6 5.0 %collective-permute-start.12 = (bf16[2,32,1024]{2,1,0:T(8,128)(2,1)S(1)}, bf16[2,32,1024]{2,1,0:T(8,128)(2,1)S(1)}, u32[]{:S(2)}, u32[]{:S(2)}) collective-permute-start(bf16[2,32,1024]{2,1,0:T(8,128)(2,1)S(1)} %fusion.32), channel_id=1, source_target_pairs={{0,16},{4,20},{8,24},{12,28},{16,0},{20,4},{24,8},{28,12},{1,17},{... | collective-permute-start | bytes 393224 | tf_op jit(solution)/shard_map/ppermute | solution.py:31
Sparse Core Ops, SparseCore 0:
  82.0 16.7 reduce-scatter.5
  101.0 17.6 reduce-scatter.3
  174.9 26.3 reduce-scatter.7
